TPU v7x, 32 devices: a whole 2x2x4 slice. The times are simulated.
32 devices in a mesh: dp: 8 (over z, y), tensor: 4 (over x, core).
Axes of the slice: x: 2, y: 2, z: 4, core: 2. Of those that a mesh axis runs over, the one named last changes fastest.
Arguments:
- tokens: bfloat16 [8192, 1024], P(('dp', 'tensor')), may hold values from -6 to 6
- cotangent: bfloat16 [8192, 1024], P(('dp', 'tensor')), may hold values from -6 to 6
- prefix: int32 [8], P('dp'), may hold values from 102 to 512
- qkv_weight: float32 [1024, 3, 1024], P('dp', None, 'tensor'), may hold values from -0.1875 to 0.1875
- qkv_moment: float32 [1024, 3, 1024], P('dp', None, 'tensor'), may hold values from -112 to 112
- qkv_square: float32 [1024, 3, 1024], P('dp', None, 'tensor'), may hold values from 24.576 to 2457.6
- out_weight: float32 [1024, 1024], P('dp', 'tensor'), may hold values from -1 to 1
- out_moment: float32 [1024, 1024], P('dp', 'tensor'), may hold values from -112 to 112
- out_square: float32 [1024, 1024], P('dp', 'tensor'), may hold values from 24.576 to 2457.6
- up_weight: float32 [1024, 4096], P('dp', 'tensor'), may hold values from -0.1875 to 0.1875
- up_moment: float32 [1024, 4096], P('dp', 'tensor'), may hold values from -112 to 112
- up_square: float32 [1024, 4096], P('dp', 'tensor'), may hold values from 24.576 to 2457.6
- down_weight: float32 [1024, 4096], P('dp', 'tensor'), may hold values from -0.09375 to 0.09375
- down_moment: float32 [1024, 4096], P('dp', 'tensor'), may hold values from -112 to 112
- down_square: float32 [1024, 4096], P('dp', 'tensor'), may hold values from 24.576 to 2457.6
- norm_gains: float32 [2, 1024], replicated, may hold values from 0.5 to 1.5
- gains_moment: float32 [2, 1024], replicated, may hold values from -256 to 256
- gains_square: float32 [2, 1024], replicated, may hold values from 245.76 to 8192
- biases: float32 [6, 1024], replicated, may hold values from -1.75 to 1.75
- biases_moment: float32 [6, 1024], replicated, may hold values from -256 to 256
- biases_square: float32 [6, 1024], replicated, may hold values from 8192 to 819200
- up_bias: float32 [4096], replicated, may hold values from -1.75 to 1.75
- up_bias_moment: float32 [4096], replicated, may hold values from -256 to 256
- up_bias_square: float32 [4096], replicated, may hold values from 245.76 to 8192
Outputs:
- output: bfloat16 [8192, 1024], P(('dp', 'tensor'))
- input_grad: float32 [8192, 1024], P(('dp', 'tensor'))
- qkv_weight_grad: float32 [1024, 3, 1024], P('dp', None, 'tensor')
- out_weight_grad: float32 [1024, 1024], P('dp', 'tensor')
- up_weight_grad: float32 [1024, 4096], P('dp', 'tensor')
- down_weight_grad: float32 [1024, 4096], P('dp', 'tensor')
- norm_gains_grad: float32 [2, 1024], replicated
- biases_grad: float32 [6, 1024], replicated
- up_bias_grad: float32 [4096], replicated
- qkv_weight_new: float32 [1024, 3, 1024], P('dp', None, 'tensor')
- out_weight_new: float32 [1024, 1024], P('dp', 'tensor')
- up_weight_new: float32 [1024, 4096], P('dp', 'tensor')
- down_weight_new: float32 [1024, 4096], P('dp', 'tensor')
- norm_gains_new: float32 [2, 1024], replicated
- biases_new: float32 [6, 1024], replicated
- up_bias_new: float32 [4096], replicated
- qkv_weight_low: bfloat16 [1024, 3, 1024], P('dp', None, 'tensor')
- out_weight_low: bfloat16 [1024, 1024], P('dp', 'tensor')
- up_weight_low: bfloat16 [1024, 4096], P('dp', 'tensor')
- down_weight_low: bfloat16 [1024, 4096], P('dp', 'tensor')
- qkv_moment_new: float32 [1024, 3, 1024], P('dp', None, 'tensor')
- out_moment_new: float32 [1024, 1024], P('dp', 'tensor')
- up_moment_new: float32 [1024, 4096], P('dp', 'tensor')
- down_moment_new: float32 [1024, 4096], P('dp', 'tensor')
- gains_moment_new: float32 [2, 1024], replicated
- biases_moment_new: float32 [6, 1024], replicated
- up_bias_moment_new: float32 [4096], replicated
- qkv_square_new: float32 [1024, 3, 1024], P('dp', None, 'tensor')
- out_square_new: float32 [1024, 1024], P('dp', 'tensor')
- up_square_new: float32 [1024, 4096], P('dp', 'tensor')
- down_square_new: float32 [1024, 4096], P('dp', 'tensor')
- gains_square_new: float32 [2, 1024], replicated
- biases_square_new: float32 [6, 1024], replicated
- up_bias_square_new: float32 [4096], replicated
- weight_norms: float32 [4], replicated
- step_norms: float32 [4], replicated
All inputs are finite; a program needn't handle non-finite values.
Results may differ from a plain program's by a relative error of at most 0.022.
Values may be sent and summed in bfloat16 or wider, within the bound.
No kernel may reach another device: no remote copies, remote signals or barrier semaphores. Data moves between devices by JAX's collectives and lax.ppermute only.
A program may use at most 128 MiB of HBM per device.

v0:
```python
import jax
import jax.numpy as jnp
from jax import lax
from jax.sharding import PartitionSpec as P

HEADS = 16
HEAD = 64
QBLOCK = 512
learn_rate = 0.5
gelu_coef = 0.7978845608028654


def norm_forward(values, gain, shift):
    mean = jnp.mean(values, axis=-1, keepdims=True)
    centred = values - mean
    inverse = lax.rsqrt(jnp.mean(centred * centred, axis=-1, keepdims=True) + 1e-05)
    unit = centred * inverse
    return (unit * gain + shift, unit, inverse)


def norm_backward(grad, unit, inverse, gain):
    scaled = grad * gain
    inner = (
        scaled
        - jnp.mean(scaled, axis=-1, keepdims=True)
        - unit * jnp.mean(scaled * unit, axis=-1, keepdims=True)
    )
    return (inverse * inner, jnp.sum(grad * unit, axis=0), jnp.sum(grad, axis=0))


def gelu_value(v):
    return 0.5 * v * (1.0 + jnp.tanh(gelu_coef * (v + 0.044715 * v * v * v)))


def gelu_slope(v):
    hyper = jnp.tanh(gelu_coef * (v + 0.044715 * v * v * v))
    return 0.5 * (1.0 + hyper) + 0.5 * v * (1.0 - hyper * hyper) * gelu_coef * (
        1.0 + 3.0 * 0.044715 * v * v
    )


def alibi_slopes():
    return jnp.exp2(-8.0 * (lax.iota(jnp.int32, HEADS) + 1).astype(jnp.float32) / HEADS)


def block_scores(queries, keys, slope, start, prefix_len, scale):
    count = queries.shape[0]
    length = keys.shape[0]
    scores = jnp.einsum("bhe,khe->hbk", queries, keys, preferred_element_type=jnp.float32) * scale
    row_pos = start + lax.iota(jnp.int32, count)
    col_pos = lax.iota(jnp.int32, length)
    offset = (col_pos[None, :] - row_pos[:, None]).astype(jnp.float32)
    scores = scores + slope[:, None, None] * offset[None]
    allowed = (col_pos[None, :] <= row_pos[:, None]) | (col_pos[None, :] < prefix_len)
    return (scores, allowed)


def place(part, width, rank):
    return lax.dynamic_update_slice(jnp.zeros((width,), jnp.float32), part, (rank * part.shape[0],))


def adam_terms(moment, square, grad):
    new_moment = 0.5 * moment + 0.5 * grad
    new_square = 0.5 * square + 0.5 * grad * grad
    return (new_moment, new_square, new_moment / (jnp.sqrt(new_square) + 1e-06))


def lamb_rows(weight, moment, square, grad):
    new_moment, new_square, direction = adam_terms(moment, square, grad)
    weight_norm = jnp.sqrt(jnp.sum(weight * weight, axis=-1, keepdims=True))
    step_norm = jnp.sqrt(jnp.sum(direction * direction, axis=-1, keepdims=True))
    return (weight - learn_rate * (weight_norm / step_norm) * direction, new_moment, new_square)


def per_device(
    tokens,
    cotangent,
    prefix,
    qkv_weight,
    qkv_moment,
    qkv_square,
    out_weight,
    out_moment,
    out_square,
    up_weight,
    up_moment,
    up_square,
    down_weight,
    down_moment,
    down_square,
    norm_gains,
    gains_moment,
    gains_square,
    biases,
    biases_moment,
    biases_square,
    up_bias,
    up_bias_moment,
    up_bias_square,
):
    rows = tokens.shape[0]
    length = rows * lax.axis_size("tensor")
    rank = lax.axis_index("tensor")
    local_width = qkv_weight.shape[2]
    local_hidden = up_weight.shape[1]
    heads_here = local_width // HEAD
    block = min(QBLOCK, length)
    blocks = length // block
    scale = float(HEAD) ** (-0.5)
    prefix_len = prefix[0]
    slope = lax.dynamic_slice_in_dim(alibi_slopes(), rank * heads_here, heads_here)
    shards = (
        qkv_weight.astype(jnp.bfloat16),
        out_weight.astype(jnp.bfloat16),
        up_weight.astype(jnp.bfloat16),
        down_weight.astype(jnp.bfloat16),
    )
    qkv_full, out_full, up_full, down_full = (
        lax.all_gather(shards[0], "dp", axis=0, tiled=True),
        lax.all_gather(shards[1], "dp", axis=0, tiled=True),
        lax.all_gather(shards[2], "dp", axis=0, tiled=True),
        lax.all_gather(shards[3], "dp", axis=0, tiled=True),
    )
    x_rows = tokens.astype(jnp.float32)
    normed, unit_one, inverse_one = norm_forward(x_rows, norm_gains[0], biases[0])
    normed_all = lax.all_gather(normed.astype(jnp.bfloat16), "tensor", axis=0, tiled=True)
    projected = jnp.einsum("ld,dce->cle", normed_all, qkv_full, preferred_element_type=jnp.float32)
    query_bias = lax.dynamic_slice_in_dim(biases[2], rank * local_width, local_width)
    value_bias = lax.dynamic_slice_in_dim(biases[3], rank * local_width, local_width)
    query_heads = (projected[0] + query_bias).astype(jnp.bfloat16).reshape(length, heads_here, HEAD)
    key_heads = projected[1].astype(jnp.bfloat16).reshape(length, heads_here, HEAD)
    value_heads = (projected[2] + value_bias).astype(jnp.bfloat16).reshape(length, heads_here, HEAD)

    def attend(block_index):
        start = block_index * block
        queries = lax.dynamic_slice_in_dim(query_heads, start, block, 0)
        scores, allowed = block_scores(queries, key_heads, slope, start, prefix_len, scale)
        scores = jnp.where(allowed[None], scores, -1e30)
        peak = jnp.max(scores, axis=-1, keepdims=True)
        expo = jnp.exp(scores - peak)
        totals = jnp.sum(expo, axis=-1, keepdims=True)
        probs = (expo / totals).astype(jnp.bfloat16)
        mixed = jnp.einsum("hbk,khe->bhe", probs, value_heads, preferred_element_type=jnp.float32)
        return (mixed.reshape(block, local_width), (peak + jnp.log(totals))[..., 0])

    mixed, logsum = lax.map(attend, lax.iota(jnp.int32, blocks))
    context_low = mixed.reshape(length, local_width).astype(jnp.bfloat16)
    piece = context_low
    attn_rows = lax.psum_scatter(
        jnp.einsum("le,de->ld", piece, out_full, preferred_element_type=jnp.float32),
        "tensor",
        scatter_dimension=0,
        tiled=True,
    )
    resid = x_rows + (attn_rows + biases[4])
    normed_two, unit_two, inverse_two = norm_forward(resid, norm_gains[1], biases[1])
    normed_two_low = normed_two.astype(jnp.bfloat16)
    normed_two_all = lax.all_gather(normed_two_low, "tensor", axis=0, tiled=True)
    up_slice = lax.dynamic_slice_in_dim(up_bias, rank * local_hidden, local_hidden)
    pre = jnp.dot(normed_two_all, up_full, preferred_element_type=jnp.float32) + up_slice
    hidden_low = gelu_value(pre).astype(jnp.bfloat16)
    piece = hidden_low
    mlp_rows = lax.psum_scatter(
        jnp.einsum("lf,df->ld", piece, down_full, preferred_element_type=jnp.float32).astype(
            jnp.bfloat16
        ),
        "tensor",
        scatter_dimension=0,
        tiled=True,
    ).astype(jnp.float32)
    output = (resid + (mlp_rows + biases[5])).astype(jnp.bfloat16)
    qkv_full, out_full, up_full, down_full = (
        lax.all_gather(shards[0], "dp", axis=0, tiled=True),
        lax.all_gather(shards[1], "dp", axis=0, tiled=True),
        lax.all_gather(shards[2], "dp", axis=0, tiled=True),
        lax.all_gather(shards[3], "dp", axis=0, tiled=True),
    )
    out_grad = cotangent.astype(jnp.float32)
    down_bias_part = jnp.sum(out_grad, axis=0)
    mlp_grad_all = lax.all_gather(cotangent, "tensor", axis=0, tiled=True)
    down_grad = jnp.einsum(
        "ld,lf->df", mlp_grad_all, hidden_low, preferred_element_type=jnp.float32
    )
    hidden_grad = jnp.dot(mlp_grad_all, down_full, preferred_element_type=jnp.float32)
    pre_grad = (hidden_grad * gelu_slope(pre)).astype(jnp.bfloat16)
    up_bias_part = place(jnp.sum(pre_grad, axis=0, dtype=jnp.float32), up_bias.shape[0], rank)
    up_grad = jnp.einsum("ld,lf->df", normed_two_all, pre_grad, preferred_element_type=jnp.float32)
    piece = pre_grad
    normed_two_grad = lax.psum_scatter(
        jnp.einsum("lf,df->ld", piece, up_full, preferred_element_type=jnp.float32),
        "tensor",
        scatter_dimension=0,
        tiled=True,
    )
    resid_from_norm, gain_two_part, shift_two_part = norm_backward(
        normed_two_grad, unit_two, inverse_two, norm_gains[1]
    )
    resid_grad = out_grad + resid_from_norm
    branch_low = resid_grad.astype(jnp.bfloat16)
    out_bias_part = jnp.sum(branch_low, axis=0, dtype=jnp.float32)
    branch_all = lax.all_gather(branch_low, "tensor", axis=0, tiled=True)
    out_weight_part = jnp.einsum(
        "ld,le->de", branch_all, context_low, preferred_element_type=jnp.float32
    )
    context_grad = jnp.dot(branch_all, out_full, preferred_element_type=jnp.float32).astype(
        jnp.bfloat16
    )
    grad_heads = context_grad.reshape(length, heads_here, HEAD)

    def attend_back(carry, block_index):
        key_grad, value_grad = carry
        start = block_index * block
        queries = lax.dynamic_slice_in_dim(query_heads, start, block, 0)
        grad_out = lax.dynamic_slice_in_dim(grad_heads, start, block, 0)
        scores, allowed = block_scores(queries, key_heads, slope, start, prefix_len, scale)
        probs = jnp.where(allowed[None], jnp.exp(scores - logsum[block_index][..., None]), 0.0)
        prob_grad = jnp.einsum(
            "bhe,khe->hbk", grad_out, value_heads, preferred_element_type=jnp.float32
        )
        delta = jnp.sum(probs * prob_grad, axis=-1, keepdims=True)
        score_grad = (probs * (prob_grad - delta)).astype(jnp.bfloat16)
        query_grad = (
            jnp.einsum("hbk,khe->bhe", score_grad, key_heads, preferred_element_type=jnp.float32)
            * scale
        )
        key_grad = (
            key_grad
            + jnp.einsum("hbk,bhe->khe", score_grad, queries, preferred_element_type=jnp.float32)
            * scale
        )
        value_grad = value_grad + jnp.einsum(
            "hbk,bhe->khe", probs.astype(jnp.bfloat16), grad_out, preferred_element_type=jnp.float32
        )
        return ((key_grad, value_grad), query_grad.reshape(block, local_width))

    empty = jnp.zeros((length, heads_here, HEAD), jnp.float32)
    (key_grad, value_grad), query_grad = lax.scan(
        attend_back, (empty, empty), lax.iota(jnp.int32, blocks)
    )
    query_low = query_grad.reshape(length, local_width).astype(jnp.bfloat16)
    key_low = key_grad.reshape(length, local_width).astype(jnp.bfloat16)
    value_low = value_grad.reshape(length, local_width).astype(jnp.bfloat16)
    stacked_grad = jnp.stack([query_low, key_low, value_low])
    qkv_part = jnp.einsum(
        "ld,cle->dce", normed_all, stacked_grad, preferred_element_type=jnp.float32
    )
    piece = stacked_grad
    normed_grad = lax.psum_scatter(
        jnp.einsum("cle,dce->ld", piece, qkv_full, preferred_element_type=jnp.float32).astype(
            jnp.bfloat16
        ),
        "tensor",
        scatter_dimension=0,
        tiled=True,
    ).astype(jnp.float32)
    input_from_norm, gain_one_part, shift_one_part = norm_backward(
        normed_grad, unit_one, inverse_one, norm_gains[0]
    )
    input_grad = resid_grad + input_from_norm
    qkv_g, out_g, up_g, down_g = (
        lax.psum_scatter(
            qkv_part.astype(jnp.bfloat16), "dp", scatter_dimension=0, tiled=True
        ).astype(jnp.float32),
        lax.psum_scatter(
            out_weight_part.astype(jnp.bfloat16), "dp", scatter_dimension=0, tiled=True
        ).astype(jnp.float32),
        lax.psum_scatter(
            up_grad.astype(jnp.bfloat16), "dp", scatter_dimension=0, tiled=True
        ).astype(jnp.float32),
        lax.psum_scatter(
            down_grad.astype(jnp.bfloat16), "dp", scatter_dimension=0, tiled=True
        ).astype(jnp.float32),
    )
    width = biases.shape[1]
    gains_part = jnp.stack([gain_one_part, gain_two_part])
    biases_part = jnp.stack(
        [
            shift_one_part,
            shift_two_part,
            place(jnp.sum(query_low, axis=0, dtype=jnp.float32), width, rank),
            place(jnp.sum(value_low, axis=0, dtype=jnp.float32), width, rank),
            out_bias_part,
            down_bias_part,
        ]
    )
    qkv_m, qkv_s, qkv_dir = adam_terms(qkv_moment, qkv_square, qkv_g)
    out_m, out_s, out_dir = adam_terms(out_moment, out_square, out_g)
    up_m, up_s, up_dir = adam_terms(up_moment, up_square, up_g)
    down_m, down_s, down_dir = adam_terms(down_moment, down_square, down_g)
    local_sums = jnp.stack(
        [
            jnp.sum(qkv_weight * qkv_weight),
            jnp.sum(qkv_dir * qkv_dir),
            jnp.sum(out_weight * out_weight),
            jnp.sum(out_dir * out_dir),
            jnp.sum(up_weight * up_weight),
            jnp.sum(up_dir * up_dir),
            jnp.sum(down_weight * down_weight),
            jnp.sum(down_dir * down_dir),
        ]
    )
    gains_g, biases_g, upb_g = lax.psum((gains_part, biases_part, up_bias_part), ("dp", "tensor"))
    totals = lax.psum(local_sums, ("dp", "tensor"))
    norms = jnp.sqrt(totals).reshape(4, 2)
    qkv_n = qkv_weight - learn_rate * (norms[0, 0] / norms[0, 1]) * qkv_dir
    out_n = out_weight - learn_rate * (norms[1, 0] / norms[1, 1]) * out_dir
    up_n = up_weight - learn_rate * (norms[2, 0] / norms[2, 1]) * up_dir
    down_n = down_weight - learn_rate * (norms[3, 0] / norms[3, 1]) * down_dir
    gains_n, gains_m, gains_s = lamb_rows(norm_gains, gains_moment, gains_square, gains_g)
    biases_n, biases_m, biases_s = lamb_rows(biases, biases_moment, biases_square, biases_g)
    upb_n, upb_m, upb_s = lamb_rows(up_bias, up_bias_moment, up_bias_square, upb_g)
    return (
        output,
        input_grad,
        qkv_g,
        out_g,
        up_g,
        down_g,
        gains_g,
        biases_g,
        upb_g,
        qkv_n,
        out_n,
        up_n,
        down_n,
        gains_n,
        biases_n,
        upb_n,
        qkv_n.astype(jnp.bfloat16),
        out_n.astype(jnp.bfloat16),
        up_n.astype(jnp.bfloat16),
        down_n.astype(jnp.bfloat16),
        qkv_m,
        out_m,
        up_m,
        down_m,
        gains_m,
        biases_m,
        upb_m,
        qkv_s,
        out_s,
        up_s,
        down_s,
        gains_s,
        biases_s,
        upb_s,
        norms[:, 0],
        norms[:, 1],
    )


def solution(mesh):
    return jax.shard_map(
        per_device,
        mesh=mesh,
        in_specs=(
            P(("dp", "tensor"), None),
            P(("dp", "tensor"), None),
            P("dp"),
            P("dp", None, "tensor"),
            P("dp", None, "tensor"),
            P("dp", None, "tensor"),
            P("dp", "tensor"),
            P("dp", "tensor"),
            P("dp", "tensor"),
            P("dp", "tensor"),
            P("dp", "tensor"),
            P("dp", "tensor"),
            P("dp", "tensor"),
            P("dp", "tensor"),
            P("dp", "tensor"),
            P(),
            P(),
            P(),
            P(),
            P(),
            P(),
            P(),
            P(),
            P(),
        ),
        out_specs=(
            P(("dp", "tensor"), None),
            P(("dp", "tensor"), None),
            P("dp", None, "tensor"),
            P("dp", "tensor"),
            P("dp", "tensor"),
            P("dp", "tensor"),
            P(),
            P(),
            P(),
            P("dp", None, "tensor"),
            P("dp", "tensor"),
            P("dp", "tensor"),
            P("dp", "tensor"),
            P(),
            P(),
            P(),
            P("dp", None, "tensor"),
            P("dp", "tensor"),
            P("dp", "tensor"),
            P("dp", "tensor"),
            P("dp", None, "tensor"),
            P("dp", "tensor"),
            P("dp", "tensor"),
            P("dp", "tensor"),
            P(),
            P(),
            P(),
            P("dp", None, "tensor"),
            P("dp", "tensor"),
            P("dp", "tensor"),
            P("dp", "tensor"),
            P(),
            P(),
            P(),
            P(),
            P(),
        ),
        check_vma=False,
    )
```

profile of v0, /device:TPU:0, one launch (start us, length us, event | category | flops | bytes accessed | tf_op | source)
XLA Modules:
  0.0 828.6 jit_solution(16726841083446359867)
XLA Ops:
  17.6 34.4 %all_gather.30 = bf16[1024,256]{1,0:T(8,128)(2,1)S(1)} all-gather(bf16[128,256]{1,0:T(8,128)(2,1)S(1)} %get-tuple-element.302), channel_id=1, replica_groups=mesh['dp'=8,'tensor'=4] {'dp'}, dimensions={0}, use_global_device_ids=true | all-gather | bytes 589824 | tf_op jit(solution)/shard_map/all_gather | solution.py:120
  52.0 10.1 %all-gather.10.cloned.1.call-done = bf16[1024,3,256]{0,2,1:T(8,128)(2,1)} async-done(((bf16[128,3,256]{0,2,1:T(8,128)(2,1)}), bf16[1024,3,256]{0,2,1:T(8,128)(2,1)}) %all-gather.10.cloned.1.call-update) | async-done | bytes 1572880 | tf_op jit(solution)/shard_map/all_gather | solution.py:119
  62.1 22.6 %all-gather.8.cloned.1.call-done = bf16[1024,1024]{1,0:T(8,128)(2,1)} async-done(((bf16[256,1024]{1,0:T(8,128)(2,1)}), bf16[1024,1024]{1,0:T(8,128)(2,1)}) %all-gather.8.cloned.1.call-update) | async-done | bytes 2097168 | tf_op jit(solution)/shard_map/all_gather | solution.py:126
  84.8 3.9 fusion.40
  89.2 23.8 %while.27 = (s32[]{:T(128)}, bf16[2,512,256]{2,1,0:T(8,128)(2,1)S(1)}, f32[2,4,512]{2,1,0:T(4,128)S(1)}, s32[2]{0:T(128)S(1)}, s32[]{:T(128)}, /*index=5*/bf16[1...) while((s32[]{:T(128)}, ...), condition=%wide.region_5.6_spmd, body=%wide.region_2.5_spmd.sunk | while | flops 576716288 | bytes 38347504 | solution.py:146
  91.8 2.8 fusion.136
  94.6 3.0 fusion.137
  97.5 3.4 fusion.138
  103.7 2.8 fusion.136
  106.5 3.0 fusion.137
  109.4 3.4 fusion.138
  113.8 3.8 fusion.86
  119.2 43.2 %reduce-scatter.9.cloned.1.call-done = f32[256,1024]{1,0:T(8,128)} async-done(((f32[1024,1024]{1,0:T(8,128)}), f32[256,1024]{1,0:T(8,128)}) %reduce-scatter.9.cloned.1.call-update) | async-done | bytes 1048592 | tf_op jit(solution)/shard_map/reduce_scatter | solution.py:149
  168.1 45.9 %all-gather.14.cloned.1.call-done = bf16[1024,1024]{1,0:T(8,128)(2,1)} async-done(((bf16[128,1024]{1,0:T(8,128)(2,1)}), bf16[1024,1024]{1,0:T(8,128)(2,1)}) %all-gather.14.cloned.1.call-update) | async-done | bytes 2097168 | tf_op jit(solution)/shard_map/all_gather | solution.py:121
  214.1 23.1 %all-gather.12.cloned.1.call-done = bf16[1024,1024]{1,0:T(8,128)(2,1)} async-done(((bf16[256,1024]{1,0:T(8,128)(2,1)}), bf16[1024,1024]{1,0:T(8,128)(2,1)}) %all-gather.12.cloned.1.call-update) | async-done | bytes 2097168 | tf_op jit(solution)/shard_map/all_gather | solution.py:158
  237.2 6.5 fusion.87
  243.7 17.5 %all-gather.18.cloned.1.call-done = bf16[1024,1024]{1,0:T(8,128)(2,1)} async-done(((bf16[256,1024]{1,0:T(8,128)(2,1)}), bf16[1024,1024]{1,0:T(8,128)(2,1)}) %all-gather.18.cloned.1.call-update) | async-done | bytes 2097168 | tf_op jit(solution)/shard_map/all_gather | solution.py:180
  261.2 51.8 %all-gather.16.cloned.1.call-done = bf16[1024,1024]{1,0:T(8,128)(2,1)} async-done(((bf16[128,1024]{1,0:T(8,128)(2,1)}), bf16[1024,1024]{1,0:T(8,128)(2,1)}) %all-gather.16.cloned.1.call-update) | async-done | bytes 2097168 | tf_op jit(solution)/shard_map/all_gather | solution.py:122
  313.0 8.7 %convert_reduce_fusion = (f32[1024]{0:T(1024)}, bf16[1024,1024]{1,0:T(8,128)(2,1)S(1)}) fusion(f32[1024,1024]{1,0:T(8,128)} %fusion.87, f32[1024]{0:T(1024)S(1)} %dynamic_slice.34, bf16[1024,1024]{1,0:T(8,128)(2,1)} %all-gather.18.cloned.1.call-done, bf16[1024,1024]{1,0:T(8,128)(2,1)} %all-gather.16.cloned.1.call-done), kind=kOutput, calls=%fused_computation.55 | convolution fusion | flops 2170551296 | bytes 10493952 | tf_op jit(solution)/shard_map/dot_general | solution.py:184
  323.0 4.3 fusion.88
  327.5 7.0 convolution_convert_fusion.1
  334.6 36.1 %reduce-scatter.13.cloned.1.call-done = f32[256,1024]{1,0:T(8,128)} async-done(((f32[1024,1024]{1,0:T(8,128)}), f32[256,1024]{1,0:T(8,128)}) %reduce-scatter.13.cloned.1.call-update) | async-done | bytes 1048592 | tf_op jit(solution)/shard_map/reduce_scatter | solution.py:189
  370.7 2.3 multiply_reduce_fusion.1
  373.0 31.4 %reduce-scatter.11.cloned.1.call-done = bf16[256,1024]{1,0:T(8,128)(2,1)} async-done(((bf16[1024,1024]{1,0:T(8,128)(2,1)}), bf16[256,1024]{1,0:T(8,128)(2,1)}) %reduce-scatter.11.cloned.1.call-update) | async-done | bytes 524304 | tf_op jit(solution)/shard_map/reduce_scatter | solution.py:163
  404.4 3.9 convert_reduce_fusion.4
  408.3 5.9 convolution_convert_fusion
  414.4 7.4 convert_bitcast_fusion
  421.8 9.2 %all-gather.20.cloned.1.call-done = bf16[1024,1024]{1,0:T(8,128)(2,1)} async-done(((bf16[256,1024]{1,0:T(8,128)(2,1)}), bf16[1024,1024]{1,0:T(8,128)(2,1)}) %all-gather.20.cloned.1.call-update) | async-done | bytes 2097168 | tf_op jit(solution)/shard_map/all_gather | solution.py:201
  431.0 3.2 convolution_convert_fusion.2
  434.5 3.2 convolution_convert_fusion.3
  437.8 32.4 %while.28 = (s32[]{:T(128)}, f32[1024,4,64]{0,2,1:T(8,128)S(1)}, f32[1024,4,64]{0,2,1:T(8,128)S(1)}, bf16[2,512,256]{1,2,0:T(8,128)(2,1)}, s32[2]{0:T(128)S(1)},...) while((s32[]{:T(128)}, f32[1024,4,64]{0,2,1:T(8,128)S(1)}, ...), condition=%wide.region_15.16_spmd.clone, body=%wide.region_13.15_spmd.clone.sunk | while | flops 1368915456 | bytes 82101112 | solution.py:237
  442.3 2.4 fusion.148
  444.7 3.9 multiply_reduce_fusion.20
  458.4 2.4 fusion.148
  460.9 3.9 multiply_reduce_fusion.20
  472.0 4.6 fusion.43
  477.0 4.6 bitcast_convert_fusion
  485.1 17.9 %reduce-scatter.21.cloned.1.call-done = bf16[128,1024]{1,0:T(8,128)(2,1)} async-done(((bf16[1024,1024]{1,0:T(8,128)(2,1)}), bf16[128,1024]{1,0:T(8,128)(2,1)}) %reduce-scatter.21.cloned.1.call-update) | async-done | bytes 262160 | tf_op jit(solution)/shard_map/reduce_scatter | solution.py:267
  503.0 3.0 multiply_reduce_fusion.7
  506.1 67.9 %reduce-scatter.23.cloned.1.call-done = bf16[128,1024]{1,0:T(8,128)(2,1)} async-done(((bf16[1024,1024]{1,0:T(8,128)(2,1)}), bf16[128,1024]{1,0:T(8,128)(2,1)}) %reduce-scatter.23.cloned.1.call-update) | async-done | bytes 262160 | tf_op jit(solution)/shard_map/reduce_scatter | solution.py:270
  573.9 2.8 multiply_reduce_fusion.5
  578.2 61.4 %reduce-scatter.19.cloned.1.call-done = bf16[128,256]{1,0:T(8,128)(2,1)} async-done(((bf16[1024,256]{1,0:T(8,128)(2,1)}), bf16[128,256]{1,0:T(8,128)(2,1)}) %reduce-scatter.19.cloned.1.call-update) | async-done | bytes 65552 | tf_op jit(solution)/shard_map/reduce_scatter | solution.py:264
  641.8 66.3 %reduce-scatter.17.cloned.1.call-done = bf16[128,3,256]{2,0,1:T(8,128)(2,1)} async-done(((bf16[1024,3,256]{2,0,1:T(8,128)(2,1)}), bf16[128,3,256]{2,0,1:T(8,128)(2,1)}) %reduce-scatter.17.cloned.1.call-update) | async-done | bytes 196624 | tf_op jit(solution)/shard_map/reduce_scatter | solution.py:261
  708.1 2.9 multiply_reduce_fusion.9
  711.0 5.8 stack.85
  716.8 23.9 %reduce-scatter.15.cloned.1.call-done = bf16[256,1024]{1,0:T(8,128)(2,1)} async-done(((bf16[1024,1024]{1,0:T(8,128)(2,1)}), bf16[256,1024]{1,0:T(8,128)(2,1)}) %reduce-scatter.15.cloned.1.call-update) | async-done | bytes 524304 | tf_op jit(solution)/shard_map/reduce_scatter | solution.py:248
  745.7 41.1 %all-reduce = (f32[2,1024]{1,0:T(2,128)}, f32[6,1024]{1,0:T(8,128)}, f32[4096]{0:T(1024)}, f32[8]{0:T(128)}) all-reduce(f32[2,1024]{1,0:T(2,128)} %pad_maximum_fusion.3, f32[6,1024]{1,0:T(8,128)} %stack.76, f32[4096]{0:T(1024)} %copy-done.30, f32[8]{0:T(128)} %stack.85), channel_id=1, replica_groups=mesh['dp'=8,'tensor'=4] {'dp','tensor'}, use_global_device_ids=true, to_apply=%region_25.26 | all-reduce | flops 12296 | bytes 98368 | tf_op jit(solution)/shard_map/psum | solution.py:302
  819.2 2.4 fusion.57
  (230 shorter events, 79.0 us)
Async XLA Ops:
  7.2 54.9 %all-gather.10.cloned.1.call-start = ((), (), s32[]{:S(2)}) async-start(), calls=%async_computation.9 | async-start | bytes 1769472 | tf_op jit(solution)/shard_map/all_gather | solution.py:119
  9.1 75.7 %all-gather.8.cloned.1.call-start = ((), (), s32[]{:S(2)}) async-start(), calls=%async_computation.8 | async-start | bytes 2621440 | tf_op jit(solution)/shard_map/all_gather | solution.py:126
  10.3 5.6 copy-start.31
  15.6 146.8 %reduce-scatter.9.cloned.1.call-start = ((), (), s32[]{:S(2)}) async-start(), calls=%async_computation.10 | async-start | bytes 5242880 | tf_op jit(solution)/shard_map/reduce_scatter | solution.py:149
  52.0 61.8 %copy-start.11 = (bf16[1024,256]{1,0:T(8,128)(2,1)}, bf16[1024,256]{1,0:T(8,128)(2,1)S(1)}, u32[]{:S(2)}) copy-start(bf16[1024,256]{1,0:T(8,128)(2,1)S(1)} %all_gather.30) | copy-start | bytes 1572868
  113.0 4.6 copy-start
  113.8 48.6 %copy-start.1 = (bf16[256,1024]{1,0:T(8,128)(2,1)S(1)}, bf16[256,1024]{1,0:T(8,128)(2,1)}, u32[]{:S(2)}) copy-start(bf16[256,1024]{1,0:T(8,128)(2,1)} %param.28) | copy-start | bytes 1572868
  117.7 48.2 %copy-start.7 = (f32[128,1024]{1,0:T(8,128)S(1)}, f32[128,1024]{1,0:T(8,128)}, u32[]{:S(2)}) copy-start(f32[128,1024]{1,0:T(8,128)} %param.40) | copy-start | bytes 1572868
  117.7 96.4 %all-gather.14.cloned.1.call-start = ((), (), s32[]{:S(2)}) async-start(), calls=%async_computation.12 | async-start | bytes 2359296 | tf_op jit(solution)/shard_map/all_gather | solution.py:121
  119.1 118.1 %all-gather.12.cloned.1.call-start = ((), (), s32[]{:S(2)}) async-start(), calls=%async_computation.11 | async-start | bytes 2621440 | tf_op jit(solution)/shard_map/all_gather | solution.py:158
  165.2 96.0 %all-gather.18.cloned.1.call-start = ((), (), s32[]{:S(2)}) async-start(), calls=%async_computation.15 | async-start | bytes 2621440 | tf_op jit(solution)/shard_map/all_gather | solution.py:180
  165.8 147.2 %all-gather.16.cloned.1.call-start = ((), (), s32[]{:S(2)}) async-start(), calls=%async_computation.13 | async-start | bytes 2359296 | tf_op jit(solution)/shard_map/all_gather | solution.py:122
  167.2 203.5 %reduce-scatter.13.cloned.1.call-start = ((), (), s32[]{:S(2)}) async-start(), calls=%async_computation.16 | async-start | bytes 5242880 | tf_op jit(solution)/shard_map/reduce_scatter | solution.py:189
  313.0 10.0 %copy-start.39 = (bf16[1024,1024]{1,0:T(8,128)(2,1)S(1)}, bf16[1024,1024]{1,0:T(8,128)(2,1)}, u32[]{:S(2)}) copy-start(bf16[1024,1024]{1,0:T(8,128)(2,1)} %all-gather.14.cloned.1.call-done) | copy-start | bytes 6291460
  327.4 77.0 %reduce-scatter.11.cloned.1.call-start = ((), (), s32[]{:S(2)}) async-start(), calls=%async_computation.14 | async-start | bytes 2621440 | tf_op jit(solution)/shard_map/reduce_scatter | solution.py:163
  334.5 69.9 %copy-start.6 = (bf16[256,1024]{1,0:T(8,128)(2,1)S(1)}, bf16[256,1024]{1,0:T(8,128)(2,1)}, u32[]{:S(2)}) copy-start(bf16[256,1024]{1,0:T(8,128)(2,1)} %param.29) | copy-start | bytes 1572868
  334.5 96.5 %all-gather.20.cloned.1.call-start = ((), (), s32[]{:S(2)}) async-start(), calls=%async_computation.17 | async-start | bytes 2621440 | tf_op jit(solution)/shard_map/all_gather | solution.py:201
  408.3 94.8 %reduce-scatter.21.cloned.1.call-start = ((), (), s32[]{:S(2)}) async-start(), calls=%async_computation.21 | async-start | bytes 2359296 | tf_op jit(solution)/shard_map/reduce_scatter | solution.py:267
  414.3 159.6 %reduce-scatter.23.cloned.1.call-start = ((), (), s32[]{:S(2)}) async-start(), calls=%async_computation.22 | async-start | bytes 2359296 | tf_op jit(solution)/shard_map/reduce_scatter | solution.py:270
  421.8 217.8 %reduce-scatter.19.cloned.1.call-start = ((), (), s32[]{:S(2)}) async-start(), calls=%async_computation.20 | async-start | bytes 589824 | tf_op jit(solution)/shard_map/reduce_scatter | solution.py:264
  434.3 273.8 %reduce-scatter.17.cloned.1.call-start = ((), (), s32[]{:S(2)}) async-start(), calls=%async_computation.19 | async-start | bytes 1769472 | tf_op jit(solution)/shard_map/reduce_scatter | solution.py:261
  476.7 5.0 copy-start.26
  476.7 6.3 copy-start.27
  476.7 6.9 copy-start.21
  476.7 7.5 copy-start.5
  476.7 8.2 copy-start.38
  476.7 26.3 %copy-start.18 = (f32[128,1024]{1,0:T(8,128)S(1)}, f32[128,1024]{1,0:T(8,128)}, u32[]{:S(2)}) copy-start(f32[128,1024]{1,0:T(8,128)} %param.39) | copy-start | bytes 1572868
  476.7 263.9 %reduce-scatter.15.cloned.1.call-start = ((), (), s32[]{:S(2)}) async-start(), calls=%async_computation.18 | async-start | bytes 2621440 | tf_op jit(solution)/shard_map/reduce_scatter | solution.py:248
  481.6 92.3 %copy-start.19 = (f32[128,1024]{1,0:T(8,128)S(1)}, f32[128,1024]{1,0:T(8,128)}, u32[]{:S(2)}) copy-start(f32[128,1024]{1,0:T(8,128)} %param.42) | copy-start | bytes 1572868
  481.6 92.3 %copy-start.20 = (f32[128,1024]{1,0:T(8,128)S(1)}, f32[128,1024]{1,0:T(8,128)}, u32[]{:S(2)}) copy-start(f32[128,1024]{1,0:T(8,128)} %param.41) | copy-start | bytes 1572868
  481.6 95.3 %copy-start.14 = (bf16[2,512,256]{1,2,0:T(8,128)(2,1)S(1)}, bf16[2,512,256]{1,2,0:T(8,128)(2,1)}, u32[]{:S(2)}) copy-start(bf16[2,512,256]{1,2,0:T(8,128)(2,1)} %get-tuple-element.150) | copy-start | bytes 1572868
  481.6 158.0 %copy-start.22 = (f32[128,256]{1,0:T(8,128)S(1)}, f32[128,256]{1,0:T(8,128)}, u32[]{:S(2)}) copy-start(f32[128,256]{1,0:T(8,128)} %param.36) | copy-start | bytes 393220
  481.6 158.0 %copy-start.23 = (f32[128,256]{1,0:T(8,128)S(1)}, f32[128,256]{1,0:T(8,128)}, u32[]{:S(2)}) copy-start(f32[128,256]{1,0:T(8,128)} %param.35) | copy-start | bytes 393220
  485.1 156.7 %copy-start.30 = (f32[4096]{0:T(1024)}, f32[4096]{0:T(1024)S(1)}, u32[]{:S(2)}) copy-start(f32[4096]{0:T(1024)S(1)} %dynamic_update_slice.24) | copy-start | bytes 49156
  485.1 255.5 %copy-start.2 = (bf16[256,1024]{1,0:T(8,128)(2,1)S(1)}, bf16[256,1024]{1,0:T(8,128)(2,1)}, u32[]{:S(2)}) copy-start(bf16[256,1024]{1,0:T(8,128)(2,1)} %param.28) | copy-start | bytes 1572868
  576.8 237.7 %copy-start.8 = (f32[128,1024]{1,0:T(8,128)S(1)}, f32[128,1024]{1,0:T(8,128)}, u32[]{:S(2)}) copy-start(f32[128,1024]{1,0:T(8,128)} %param.40) | copy-start | bytes 1572868
  578.2 63.6 %copy-start.33 = (f32[1,1024]{1,0:T(1,128)}, f32[1,1024]{1,0:T(1,128)S(1)}, u32[]{:S(2)}) copy-start(f32[1,1024]{1,0:T(1,128)S(1)} %constant_dynamic-update-slice_fusion.1) | copy-start | bytes 12292
  641.8 175.0 %copy-start.17 = (f32[128,256]{1,0:T(8,128)}, f32[128,256]{1,0:T(8,128)S(1)}, u32[]{:S(2)}) copy-start(f32[128,256]{1,0:T(8,128)S(1)} %get-tuple-element.275) | copy-start | bytes 393220
  641.8 175.0 %copy-start.10 = (f32[128,1024]{1,0:T(8,128)S(1)}, f32[128,1024]{1,0:T(8,128)}, u32[]{:S(2)}) copy-start(f32[128,1024]{1,0:T(8,128)} %param.37) | copy-start | bytes 1572868
  711.0 108.1 %copy-start.15 = (f32[128,3,256]{2,0,1:T(8,128)}, f32[128,3,256]{2,0,1:T(8,128)S(1)}, u32[]{:S(2)}) copy-start(f32[128,3,256]{2,0,1:T(8,128)S(1)} %get-tuple-element.279) | copy-start | bytes 1179652
  742.9 76.2 %copy-start.4 = (f32[256,1024]{1,0:T(8,128)S(1)}, f32[256,1024]{1,0:T(8,128)}, u32[]{:S(2)}) copy-start(f32[256,1024]{1,0:T(8,128)} %get-tuple-element.284) | copy-start | bytes 3145732
  806.4 12.8 %copy-start.29 = (f32[1,1024]{1,0:T(1,128)S(1)}, f32[1,1024]{1,0:T(1,128)}, u32[]{:S(2)}) copy-start(f32[1,1024]{1,0:T(1,128)} %copy-done.28) | copy-start | bytes 12292
  806.4 12.8 %copy-start.32 = (f32[256]{0:T(256)S(1)}, f32[256]{0:T(256)}, u32[]{:S(2)}) copy-start(f32[256]{0:T(256)} %copy-done.31) | copy-start | bytes 3076
  806.4 12.8 %copy-start.35 = (f32[256]{0:T(256)S(1)}, f32[256]{0:T(256)}, u32[]{:S(2)}) copy-start(f32[256]{0:T(256)} %copy-done.34) | copy-start | bytes 3076
  806.4 12.8 %copy-start.36 = (f32[256]{0:T(256)S(1)}, f32[256]{0:T(256)}, u32[]{:S(2)}) copy-start(f32[256]{0:T(256)} %broadcast_multiply_fusion) | copy-start | bytes 3076
  806.4 12.8 %copy-start.37 = (f32[256]{0:T(256)S(1)}, f32[256]{0:T(256)}, u32[]{:S(2)}) copy-start(f32[256]{0:T(256)} %broadcast_multiply_fusion.1) | copy-start | bytes 3076
  807.3 14.3 %copy-start.24 = (f32[6,1024]{1,0:T(8,128)}, f32[6,1024]{1,0:T(8,128)S(1)}, u32[]{:S(2)}) copy-start(f32[6,1024]{1,0:T(8,128)S(1)} %get-tuple-element.260) | copy-start | bytes 73732
  807.3 14.3 %copy-start.25 = (f32[6,1024]{1,0:T(8,128)}, f32[6,1024]{1,0:T(8,128)S(1)}, u32[]{:S(2)}) copy-start(f32[6,1024]{1,0:T(8,128)S(1)} %get-tuple-element.261) | copy-start | bytes 73732
  (11 other events, 19.5 us)
Sparse Core Ops, SparseCore 0:
  10.6 51.4 all-gather.9
  64.3 20.4 all-gather.7
  117.8 44.5 reduce-scatter.8
  165.0 49.0 all-gather.13
  216.1 21.0 all-gather.11
  238.6 22.5 all-gather.17
  263.9 49.0 all-gather.15
  327.5 43.1 reduce-scatter.12
  373.2 31.1 reduce-scatter.10
  408.4 22.5 all-gather.19
  434.6 68.4 reduce-scatter.20
  506.4 67.4 reduce-scatter.22
  577.8 61.7 reduce-scatter.18
  642.9 65.1 reduce-scatter.16
  710.5 30.1 reduce-scatter.14
where the time goes:
time: 839 us; the launch traced here: 829 us
  waiting for transfers between devices  529 us (63%)
  matrix products  94.9 us (11%)
  blocking collectives  75.5 us (9%)
  other arithmetic  71.6 us (9%)
  local copies, waits for them, and re-layouts  27.6 us (3%)
  between operations  21.6 us (3%)
    reduce_scatter x1, waiting for transfers between devices, per_device(): lax.psum_scatter(down_grad.astype(jnp.bfloat16), 'dp', scatter_dimension=...  67.9 us
    reduce_scatter x1, waiting for transfers between devices, per_device(): lax.psum_scatter(qkv_part.astype(jnp.bfloat16), 'dp', scatter_dimension=0...  66.3 us
    reduce_scatter x1, waiting for transfers between devices, per_device(): lax.psum_scatter(out_weight_part.astype(jnp.bfloat16), 'dp', scatter_dime...  61.4 us
    all_gather x1, waiting for transfers between devices, per_device(): lax.all_gather(shards[3], 'dp', axis=0, tiled=True)  51.8 us
    all_gather x1, waiting for transfers between devices, per_device(): lax.all_gather(shards[2], 'dp', axis=0, tiled=True)  45.9 us
    reduce_scatter x1, waiting for transfers between devices, per_device(): lax.psum_scatter(jnp.einsum('le,de->ld', piece, out_full, preferred_eleme...  43.2 us
    psum x1, blocking collectives, per_device(): lax.psum((gains_part, biases_part, up_bias_part), ('dp', 'tensor'))  41.1 us
    reduce_scatter x1, waiting for transfers between devices, per_device(): lax.psum_scatter(jnp.einsum('lf,df->ld', piece, up_full, preferred_elemen...  36.1 us
  transfers between devices with their start and end apart: 15, of which 15 were waited for; matrix products, arithmetic and copies ran while one was open for 13% of the time, Pallas kernels for 0%

commit v1 on v0

--- a/solution.py
+++ b/solution.py
@@ -8,6 +8,19 @@
 QBLOCK = 512
 learn_rate = 0.5
 gelu_coef = 0.7978845608028654
+
+
+def gather_around(array, axis, dim):
+    size, here, span = (lax.axis_size(axis), lax.axis_index(axis), array.shape[dim])
+    upward = [(i, (i + 1) % size) for i in range(size)]
+    out = jnp.zeros((*array.shape[:dim], size * span, *array.shape[dim + 1 :]), array.dtype)
+    held = array
+    for turn in range(size):
+        owner = (here - turn) % size
+        out = lax.dynamic_update_slice_in_dim(out, held, owner * span, axis=dim)
+        if turn < size - 1:
+            held = lax.ppermute(held, axis, upward)
+    return out
 
 
 def norm_forward(values, gain, shift):
@@ -155,7 +168,7 @@
     resid = x_rows + (attn_rows + biases[4])
     normed_two, unit_two, inverse_two = norm_forward(resid, norm_gains[1], biases[1])
     normed_two_low = normed_two.astype(jnp.bfloat16)
-    normed_two_all = lax.all_gather(normed_two_low, "tensor", axis=0, tiled=True)
+    normed_two_all = gather_around(normed_two_low, "tensor", 0)
     up_slice = lax.dynamic_slice_in_dim(up_bias, rank * local_hidden, local_hidden)
     pre = jnp.dot(normed_two_all, up_full, preferred_element_type=jnp.float32) + up_slice
     hidden_low = gelu_value(pre).astype(jnp.bfloat16)

time: 839 us -> 814 us (0.970)
  waiting for transfers between devices: 529 us -> 500 us
    all_gather x1, waiting for transfers between devices: 45.9 us -> 19.4 us  [per_device(): lax.all_gather(shards[2], 'dp', axis=0, tiled=True)]
    ppermute x0 -> x3, waiting for transfers between devices: none -> 23.5 us  [gather_around(): held = lax.ppermute(held, axis, upward)]
    all_gather x1 -> x0, waiting for transfers between devices: 23.1 us -> none  [per_device(): lax.all_gather(normed_two_low, 'tensor', axis=0, tiled=True)]
  transfers between devices with their start and end apart: 15 -> 17, of which waited for: 15 -> 17; matrix products, arithmetic and copies ran while one was open for 13% -> 14% of each run, Pallas kernels for 0% -> 0%
where the time goes in v1:
time: 814 us; the launch traced here: 804 us
  waiting for transfers between devices  500 us (61%)
  matrix products  94.3 us (12%)
  blocking collectives  75.6 us (9%)
  other arithmetic  71.6 us (9%)
  local copies, waits for them, and re-layouts  32.8 us (4%)
  between operations  21.7 us (3%)
    reduce_scatter x1, waiting for transfers between devices, per_device(): lax.psum_scatter(down_grad.astype(jnp.bfloat16), 'dp', scatter_dimension=...  68 us
    reduce_scatter x1, waiting for transfers between devices, per_device(): lax.psum_scatter(qkv_part.astype(jnp.bfloat16), 'dp', scatter_dimension=0...  66.6 us
    reduce_scatter x1, waiting for transfers between devices, per_device(): lax.psum_scatter(out_weight_part.astype(jnp.bfloat16), 'dp', scatter_dime...  61.3 us
    all_gather x1, waiting for transfers between devices, per_device(): lax.all_gather(shards[3], 'dp', axis=0, tiled=True)  51.7 us
    reduce_scatter x1, waiting for transfers between devices, per_device(): lax.psum_scatter(jnp.einsum('le,de->ld', piece, out_full, preferred_eleme...  41.2 us
    psum x1, blocking collectives, per_device(): lax.psum((gains_part, biases_part, up_bias_part), ('dp', 'tensor'))  41.1 us
    reduce_scatter x1, waiting for transfers between devices, per_device(): lax.psum_scatter(jnp.einsum('lf,df->ld', piece, up_full, preferred_elemen...  36.1 us
    all_gather x1, blocking collectives, per_device(): lax.all_gather(shards[1], 'dp', axis=0, tiled=True)  34.5 us
  transfers between devices with their start and end apart: 17, of which 17 were waited for; matrix products, arithmetic and copies ran while one was open for 14% of the time, Pallas kernels for 0%

profile of v1, /device:TPU:0, one launch (start us, length us, event | category | flops | bytes accessed | tf_op | source)
XLA Modules:
  0.0 803.7 jit_solution(2713885596839587949)
XLA Ops:
  17.6 34.5 %all_gather.27 = bf16[1024,256]{1,0:T(8,128)(2,1)S(1)} all-gather(bf16[128,256]{1,0:T(8,128)(2,1)S(1)} %get-tuple-element.304), channel_id=1, replica_groups=mesh['dp'=8,'tensor'=4] {'dp'}, dimensions={0}, use_global_device_ids=true | all-gather | bytes 589824 | tf_op jit(solution)/shard_map/all_gather | solution.py:133
  52.1 10.1 %all-gather.9.cloned.1.call-done = bf16[1024,3,256]{0,2,1:T(8,128)(2,1)} async-done(((bf16[128,3,256]{0,2,1:T(8,128)(2,1)}), bf16[1024,3,256]{0,2,1:T(8,128)(2,1)}) %all-gather.9.cloned.1.call-update) | async-done | bytes 1572880 | tf_op jit(solution)/shard_map/all_gather | solution.py:132
  62.2 22.6 %all-gather.7.cloned.1.call-done = bf16[1024,1024]{1,0:T(8,128)(2,1)} async-done(((bf16[256,1024]{1,0:T(8,128)(2,1)}), bf16[1024,1024]{1,0:T(8,128)(2,1)}) %all-gather.7.cloned.1.call-update) | async-done | bytes 2097168 | tf_op jit(solution)/shard_map/all_gather | solution.py:139
  84.7 3.9 fusion.40
  89.2 23.8 %while.27 = (s32[]{:T(128)}, bf16[2,512,256]{2,1,0:T(8,128)(2,1)S(1)}, f32[2,4,512]{2,1,0:T(4,128)S(1)}, s32[2]{0:T(128)S(1)}, s32[]{:T(128)}, /*index=5*/bf16[1...) while((s32[]{:T(128)}, ...), condition=%wide.region_5.6_spmd, body=%wide.region_2.5_spmd.sunk | while | flops 576716288 | bytes 38347504 | solution.py:159
  91.7 2.8 fusion.138
  94.5 3.0 fusion.139
  97.5 3.4 fusion.140
  103.6 2.8 fusion.138
  106.4 3.0 fusion.139
  109.4 3.4 fusion.140
  113.8 3.8 fusion.88
  121.2 41.2 %reduce-scatter.9.cloned.1.call-done = f32[256,1024]{1,0:T(8,128)} async-done(((f32[1024,1024]{1,0:T(8,128)}), f32[256,1024]{1,0:T(8,128)}) %reduce-scatter.9.cloned.1.call-update) | async-done | bytes 1048592 | tf_op jit(solution)/shard_map/reduce_scatter | solution.py:162
  166.6 8.6 %collective-permute-done = bf16[256,1024]{1,0:T(8,128)(2,1)S(1)} collective-permute-done((bf16[256,1024]{1,0:T(8,128)(2,1)S(1)}, bf16[256,1024]{1,0:T(8,128)(2,1)S(1)}, u32[]{:S(2)}, u32[]{:S(2)}) %collective-permute-start) | collective-permute-done | bytes 524320 | tf_op jit(solution)/shard_map/ppermute | solution.py:22
  175.2 8.6 %collective-permute-done.1 = bf16[256,1024]{1,0:T(8,128)(2,1)S(1)} collective-permute-done((bf16[256,1024]{1,0:T(8,128)(2,1)S(1)}, bf16[256,1024]{1,0:T(8,128)(2,1)S(1)}, u32[]{:S(2)}, u32[]{:S(2)}) %collective-permute-start.1) | collective-permute-done | bytes 524320 | tf_op jit(solution)/shard_map/ppermute | solution.py:22
  186.4 6.3 collective-permute-done.2
  194.6 19.4 %all-gather.11.cloned.1.call-done = bf16[1024,1024]{1,0:T(8,128)(2,1)} async-done(((bf16[128,1024]{1,0:T(8,128)(2,1)}), bf16[1024,1024]{1,0:T(8,128)(2,1)}) %all-gather.11.cloned.1.call-update) | async-done | bytes 2097168 | tf_op jit(solution)/shard_map/all_gather | solution.py:134
  214.0 6.5 fusion.89
  220.5 16.0 %all-gather.15.cloned.1.call-done = bf16[1024,1024]{1,0:T(8,128)(2,1)} async-done(((bf16[256,1024]{1,0:T(8,128)(2,1)}), bf16[1024,1024]{1,0:T(8,128)(2,1)}) %all-gather.15.cloned.1.call-update) | async-done | bytes 2097168 | tf_op jit(solution)/shard_map/all_gather | solution.py:193
  236.5 51.7 %all-gather.13.cloned.1.call-done = bf16[1024,1024]{1,0:T(8,128)(2,1)} async-done(((bf16[128,1024]{1,0:T(8,128)(2,1)}), bf16[1024,1024]{1,0:T(8,128)(2,1)}) %all-gather.13.cloned.1.call-update) | async-done | bytes 2097168 | tf_op jit(solution)/shard_map/all_gather | solution.py:135
  288.2 8.7 %convert_reduce_fusion = (f32[1024]{0:T(1024)}, bf16[1024,1024]{1,0:T(8,128)(2,1)S(1)}) fusion(f32[1024,1024]{1,0:T(8,128)} %fusion.89, f32[1024]{0:T(1024)S(1)} %dynamic_slice.34, bf16[1024,1024]{1,0:T(8,128)(2,1)} %all-gather.15.cloned.1.call-done, bf16[1024,1024]{1,0:T(8,128)(2,1)} %all-gather.13.cloned.1.call-done), kind=kOutput, calls=%fused_computation.55 | convolution fusion | flops 2170551296 | bytes 10493952 | tf_op jit(solution)/shard_map/dot_general | solution.py:197
  298.3 4.3 fusion.90
  302.7 7.0 convolution_convert_fusion.1
  309.8 36.1 %reduce-scatter.13.cloned.1.call-done = f32[256,1024]{1,0:T(8,128)} async-done(((f32[1024,1024]{1,0:T(8,128)}), f32[256,1024]{1,0:T(8,128)}) %reduce-scatter.13.cloned.1.call-update) | async-done | bytes 1048592 | tf_op jit(solution)/shard_map/reduce_scatter | solution.py:202
  348.2 31.4 %reduce-scatter.11.cloned.1.call-done = bf16[256,1024]{1,0:T(8,128)(2,1)} async-done(((bf16[1024,1024]{1,0:T(8,128)(2,1)}), bf16[256,1024]{1,0:T(8,128)(2,1)}) %reduce-scatter.11.cloned.1.call-update) | async-done | bytes 524304 | tf_op jit(solution)/shard_map/reduce_scatter | solution.py:176
  379.6 3.9 convert_reduce_fusion.4
  383.8 6.1 convolution_convert_fusion
  389.9 6.6 convert_bitcast_fusion
  396.7 9.5 %all-gather.17.cloned.1.call-done = bf16[1024,1024]{1,0:T(8,128)(2,1)} async-done(((bf16[256,1024]{1,0:T(8,128)(2,1)}), bf16[1024,1024]{1,0:T(8,128)(2,1)}) %all-gather.17.cloned.1.call-update) | async-done | bytes 2097168 | tf_op jit(solution)/shard_map/all_gather | solution.py:214
  406.2 3.2 convolution_convert_fusion.2
  409.5 3.2 convolution_convert_fusion.3
  412.8 32.4 %while.28 = (s32[]{:T(128)}, f32[1024,4,64]{0,2,1:T(8,128)S(1)}, f32[1024,4,64]{0,2,1:T(8,128)S(1)}, bf16[2,512,256]{1,2,0:T(8,128)(2,1)}, s32[2]{0:T(128)S(1)},...) while((s32[]{:T(128)}, f32[1024,4,64]{0,2,1:T(8,128)S(1)}, ...), condition=%wide.region_15.16_spmd.clone, body=%wide.region_13.15_spmd.clone.sunk | while | flops 1368915456 | bytes 82101112 | solution.py:250
  417.2 2.4 fusion.150
  419.7 3.9 multiply_reduce_fusion.20
  433.5 2.4 fusion.150
  435.9 3.9 multiply_reduce_fusion.20
  447.1 4.6 fusion.43
  452.1 4.6 bitcast_convert_fusion
  460.2 17.8 %reduce-scatter.21.cloned.1.call-done = bf16[128,1024]{1,0:T(8,128)(2,1)} async-done(((bf16[1024,1024]{1,0:T(8,128)(2,1)}), bf16[128,1024]{1,0:T(8,128)(2,1)}) %reduce-scatter.21.cloned.1.call-update) | async-done | bytes 262160 | tf_op jit(solution)/shard_map/reduce_scatter | solution.py:280
  478.1 3.0 multiply_reduce_fusion.7
  481.1 68.0 %reduce-scatter.23.cloned.1.call-done = bf16[128,1024]{1,0:T(8,128)(2,1)} async-done(((bf16[1024,1024]{1,0:T(8,128)(2,1)}), bf16[128,1024]{1,0:T(8,128)(2,1)}) %reduce-scatter.23.cloned.1.call-update) | async-done | bytes 262160 | tf_op jit(solution)/shard_map/reduce_scatter | solution.py:283
  549.1 2.8 multiply_reduce_fusion.5
  553.3 61.3 %reduce-scatter.19.cloned.1.call-done = bf16[128,256]{1,0:T(8,128)(2,1)} async-done(((bf16[1024,256]{1,0:T(8,128)(2,1)}), bf16[128,256]{1,0:T(8,128)(2,1)}) %reduce-scatter.19.cloned.1.call-update) | async-done | bytes 65552 | tf_op jit(solution)/shard_map/reduce_scatter | solution.py:277
  616.8 66.6 %reduce-scatter.17.cloned.1.call-done = bf16[128,3,256]{2,0,1:T(8,128)(2,1)} async-done(((bf16[1024,3,256]{2,0,1:T(8,128)(2,1)}), bf16[128,3,256]{2,0,1:T(8,128)(2,1)}) %reduce-scatter.17.cloned.1.call-update) | async-done | bytes 196624 | tf_op jit(solution)/shard_map/reduce_scatter | solution.py:274
  683.4 2.9 multiply_reduce_fusion.9
  686.3 5.8 stack.85
  692.1 23.7 %reduce-scatter.15.cloned.1.call-done = bf16[256,1024]{1,0:T(8,128)(2,1)} async-done(((bf16[1024,1024]{1,0:T(8,128)(2,1)}), bf16[256,1024]{1,0:T(8,128)(2,1)}) %reduce-scatter.15.cloned.1.call-update) | async-done | bytes 524304 | tf_op jit(solution)/shard_map/reduce_scatter | solution.py:261
  720.8 41.1 %all-reduce = (f32[2,1024]{1,0:T(2,128)}, f32[6,1024]{1,0:T(8,128)}, f32[4096]{0:T(1024)}, f32[8]{0:T(128)}) all-reduce(f32[2,1024]{1,0:T(2,128)} %pad_maximum_fusion.3, f32[6,1024]{1,0:T(8,128)} %stack.76, f32[4096]{0:T(1024)} %copy-done.30, f32[8]{0:T(128)} %stack.85), channel_id=1, replica_groups=mesh['dp'=8,'tensor'=4] {'dp','tensor'}, use_global_device_ids=true, to_apply=%region_25.26 | all-reduce | flops 12296 | bytes 98368 | tf_op jit(solution)/shard_map/psum | solution.py:315
  (239 shorter events, 88.8 us)
Async XLA Ops:
  7.2 55.0 %all-gather.9.cloned.1.call-start = ((), (), s32[]{:S(2)}) async-start(), calls=%async_computation.9 | async-start | bytes 1769472 | tf_op jit(solution)/shard_map/all_gather | solution.py:132
  9.1 75.6 %all-gather.7.cloned.1.call-start = ((), (), s32[]{:S(2)}) async-start(), calls=%async_computation.8 | async-start | bytes 2621440 | tf_op jit(solution)/shard_map/all_gather | solution.py:139
  11.7 76.9 %copy-start.34 = (f32[256]{0:T(256)}, f32[256]{0:T(256)S(1)}, u32[]{:S(2)}) copy-start(f32[256]{0:T(256)S(1)} %add_rsqrt_fusion.1) | copy-start | bytes 3076
  15.6 146.7 %reduce-scatter.9.cloned.1.call-start = ((), (), s32[]{:S(2)}) async-start(), calls=%async_computation.10 | async-start | bytes 5242880 | tf_op jit(solution)/shard_map/reduce_scatter | solution.py:162
  52.1 61.7 %copy-start.11 = (bf16[1024,256]{1,0:T(8,128)(2,1)}, bf16[1024,256]{1,0:T(8,128)(2,1)S(1)}, u32[]{:S(2)}) copy-start(bf16[1024,256]{1,0:T(8,128)(2,1)S(1)} %all_gather.27) | copy-start | bytes 1572868
  117.6 44.8 %copy-start.1 = (bf16[256,1024]{1,0:T(8,128)(2,1)S(1)}, bf16[256,1024]{1,0:T(8,128)(2,1)}, u32[]{:S(2)}) copy-start(bf16[256,1024]{1,0:T(8,128)(2,1)} %param.28) | copy-start | bytes 1572868
  117.6 96.4 %all-gather.11.cloned.1.call-start = ((), (), s32[]{:S(2)}) async-start(), calls=%async_computation.11 | async-start | bytes 2359296 | tf_op jit(solution)/shard_map/all_gather | solution.py:134
  119.0 117.5 %all-gather.15.cloned.1.call-start = ((), (), s32[]{:S(2)}) async-start(), calls=%async_computation.14 | async-start | bytes 2621440 | tf_op jit(solution)/shard_map/all_gather | solution.py:193
  119.6 168.6 %all-gather.13.cloned.1.call-start = ((), (), s32[]{:S(2)}) async-start(), calls=%async_computation.12 | async-start | bytes 2359296 | tf_op jit(solution)/shard_map/all_gather | solution.py:135
  121.1 224.8 %reduce-scatter.13.cloned.1.call-start = ((), (), s32[]{:S(2)}) async-start(), calls=%async_computation.15 | async-start | bytes 5242880 | tf_op jit(solution)/shard_map/reduce_scatter | solution.py:202
  166.6 8.6 %collective-permute-start = (bf16[256,1024]{1,0:T(8,128)(2,1)S(1)}, bf16[256,1024]{1,0:T(8,128)(2,1)S(1)}, u32[]{:S(2)}, u32[]{:S(2)}) collective-permute-start(bf16[256,1024]{1,0:T(8,128)(2,1)S(1)} %get-tuple-element.288), channel_id=1, source_target_pairs={{0,1},{1,2},{2,3},{3,0},{4,5},{5,6},{6,7},{7,4},{8,9},{9,10},{10,1... | collective-permute-start | bytes 1572872 | tf_op jit(solution)/shard_map/ppermute | solution.py:22
  175.2 8.6 %collective-permute-start.1 = (bf16[256,1024]{1,0:T(8,128)(2,1)S(1)}, bf16[256,1024]{1,0:T(8,128)(2,1)S(1)}, u32[]{:S(2)}, u32[]{:S(2)}) collective-permute-start(bf16[256,1024]{1,0:T(8,128)(2,1)S(1)} %collective-permute-done), channel_id=1, source_target_pairs={{0,1},{1,2},{2,3},{3,0},{4,5},{5,6},{6,7},{7,4},{8,9},{9,10},{10,1... | collective-permute-start | bytes 1572872 | tf_op jit(solution)/shard_map/ppermute | solution.py:22
  183.9 8.9 %collective-permute-start.2 = (bf16[256,1024]{1,0:T(8,128)(2,1)S(1)}, bf16[256,1024]{1,0:T(8,128)(2,1)}, u32[]{:S(2)}, u32[]{:S(2)}) collective-permute-start(bf16[256,1024]{1,0:T(8,128)(2,1)S(1)} %collective-permute-done.1), channel_id=1, source_target_pairs={{0,1},{1,2},{2,3},{3,0},{4,5},{5,6},{6,7},{7,4},{8,9},{9,10},{10,1... | collective-permute-start | bytes 1572872 | tf_op jit(solution)/shard_map/ppermute | solution.py:22
  288.2 10.0 %copy-start.40 = (bf16[1024,1024]{1,0:T(8,128)(2,1)S(1)}, bf16[1024,1024]{1,0:T(8,128)(2,1)}, u32[]{:S(2)}) copy-start(bf16[1024,1024]{1,0:T(8,128)(2,1)} %all-gather.11.cloned.1.call-done) | copy-start | bytes 6291460
  302.6 77.0 %reduce-scatter.11.cloned.1.call-start = ((), (), s32[]{:S(2)}) async-start(), calls=%async_computation.13 | async-start | bytes 2621440 | tf_op jit(solution)/shard_map/reduce_scatter | solution.py:176
  309.7 69.9 %copy-start.6 = (bf16[256,1024]{1,0:T(8,128)(2,1)S(1)}, bf16[256,1024]{1,0:T(8,128)(2,1)}, u32[]{:S(2)}) copy-start(bf16[256,1024]{1,0:T(8,128)(2,1)} %param.29) | copy-start | bytes 1572868
  309.7 96.5 %all-gather.17.cloned.1.call-start = ((), (), s32[]{:S(2)}) async-start(), calls=%async_computation.16 | async-start | bytes 2621440 | tf_op jit(solution)/shard_map/all_gather | solution.py:214
  383.5 6.4 copy-start.39
  383.5 94.5 %reduce-scatter.21.cloned.1.call-start = ((), (), s32[]{:S(2)}) async-start(), calls=%async_computation.20 | async-start | bytes 2359296 | tf_op jit(solution)/shard_map/reduce_scatter | solution.py:280
  389.9 159.2 %reduce-scatter.23.cloned.1.call-start = ((), (), s32[]{:S(2)}) async-start(), calls=%async_computation.21 | async-start | bytes 2359296 | tf_op jit(solution)/shard_map/reduce_scatter | solution.py:283
  396.6 218.0 %reduce-scatter.19.cloned.1.call-start = ((), (), s32[]{:S(2)}) async-start(), calls=%async_computation.19 | async-start | bytes 589824 | tf_op jit(solution)/shard_map/reduce_scatter | solution.py:277
  409.5 274.0 %reduce-scatter.17.cloned.1.call-start = ((), (), s32[]{:S(2)}) async-start(), calls=%async_computation.18 | async-start | bytes 1769472 | tf_op jit(solution)/shard_map/reduce_scatter | solution.py:274
  451.7 6.3 copy-start.27
  451.7 6.9 copy-start.21
  451.8 7.5 copy-start.5
  451.8 8.2 %copy-start.38 = (f32[1024]{0:T(1024)S(1)}, f32[1024]{0:T(1024)}, u32[]{:S(2)}) copy-start(f32[1024]{0:T(1024)} %get-tuple-element.321) | copy-start | bytes 12292
  451.8 26.3 %copy-start.18 = (f32[128,1024]{1,0:T(8,128)S(1)}, f32[128,1024]{1,0:T(8,128)}, u32[]{:S(2)}) copy-start(f32[128,1024]{1,0:T(8,128)} %param.39) | copy-start | bytes 1572868
  451.8 264.0 %reduce-scatter.15.cloned.1.call-start = ((), (), s32[]{:S(2)}) async-start(), calls=%async_computation.17 | async-start | bytes 2621440 | tf_op jit(solution)/shard_map/reduce_scatter | solution.py:261
  456.7 92.4 %copy-start.19 = (f32[128,1024]{1,0:T(8,128)S(1)}, f32[128,1024]{1,0:T(8,128)}, u32[]{:S(2)}) copy-start(f32[128,1024]{1,0:T(8,128)} %param.42) | copy-start | bytes 1572868
  456.7 92.4 %copy-start.20 = (f32[128,1024]{1,0:T(8,128)S(1)}, f32[128,1024]{1,0:T(8,128)}, u32[]{:S(2)}) copy-start(f32[128,1024]{1,0:T(8,128)} %param.41) | copy-start | bytes 1572868
  456.7 95.4 %copy-start.14 = (bf16[2,512,256]{1,2,0:T(8,128)(2,1)S(1)}, bf16[2,512,256]{1,2,0:T(8,128)(2,1)}, u32[]{:S(2)}) copy-start(bf16[2,512,256]{1,2,0:T(8,128)(2,1)} %get-tuple-element.150) | copy-start | bytes 1572868
  456.7 158.0 %copy-start.22 = (f32[128,256]{1,0:T(8,128)S(1)}, f32[128,256]{1,0:T(8,128)}, u32[]{:S(2)}) copy-start(f32[128,256]{1,0:T(8,128)} %param.36) | copy-start | bytes 393220
  456.7 158.0 %copy-start.23 = (f32[128,256]{1,0:T(8,128)S(1)}, f32[128,256]{1,0:T(8,128)}, u32[]{:S(2)}) copy-start(f32[128,256]{1,0:T(8,128)} %param.35) | copy-start | bytes 393220
  460.2 156.6 %copy-start.30 = (f32[4096]{0:T(1024)}, f32[4096]{0:T(1024)S(1)}, u32[]{:S(2)}) copy-start(f32[4096]{0:T(1024)S(1)} %dynamic_update_slice.40) | copy-start | bytes 49156
  460.2 255.6 %copy-start.2 = (bf16[256,1024]{1,0:T(8,128)(2,1)S(1)}, bf16[256,1024]{1,0:T(8,128)(2,1)}, u32[]{:S(2)}) copy-start(bf16[256,1024]{1,0:T(8,128)(2,1)} %param.28) | copy-start | bytes 1572868
  551.9 237.7 %copy-start.8 = (f32[128,1024]{1,0:T(8,128)S(1)}, f32[128,1024]{1,0:T(8,128)}, u32[]{:S(2)}) copy-start(f32[128,1024]{1,0:T(8,128)} %param.40) | copy-start | bytes 1572868
  553.3 63.5 %copy-start.33 = (f32[1,1024]{1,0:T(1,128)}, f32[1,1024]{1,0:T(1,128)S(1)}, u32[]{:S(2)}) copy-start(f32[1,1024]{1,0:T(1,128)S(1)} %constant_dynamic-update-slice_fusion.1) | copy-start | bytes 12292
  616.8 175.1 %copy-start.17 = (f32[128,256]{1,0:T(8,128)}, f32[128,256]{1,0:T(8,128)S(1)}, u32[]{:S(2)}) copy-start(f32[128,256]{1,0:T(8,128)S(1)} %get-tuple-element.275) | copy-start | bytes 393220
  616.8 175.1 %copy-start.10 = (f32[128,1024]{1,0:T(8,128)S(1)}, f32[128,1024]{1,0:T(8,128)}, u32[]{:S(2)}) copy-start(f32[128,1024]{1,0:T(8,128)} %param.37) | copy-start | bytes 1572868
  686.3 107.9 %copy-start.15 = (f32[128,3,256]{2,0,1:T(8,128)}, f32[128,3,256]{2,0,1:T(8,128)S(1)}, u32[]{:S(2)}) copy-start(f32[128,3,256]{2,0,1:T(8,128)S(1)} %get-tuple-element.279) | copy-start | bytes 1179652
  718.0 76.2 %copy-start.4 = (f32[256,1024]{1,0:T(8,128)S(1)}, f32[256,1024]{1,0:T(8,128)}, u32[]{:S(2)}) copy-start(f32[256,1024]{1,0:T(8,128)} %get-tuple-element.284) | copy-start | bytes 3145732
  781.5 12.8 %copy-start.29 = (f32[1,1024]{1,0:T(1,128)S(1)}, f32[1,1024]{1,0:T(1,128)}, u32[]{:S(2)}) copy-start(f32[1,1024]{1,0:T(1,128)} %copy-done.28) | copy-start | bytes 12292
  781.5 12.8 %copy-start.32 = (f32[256]{0:T(256)S(1)}, f32[256]{0:T(256)}, u32[]{:S(2)}) copy-start(f32[256]{0:T(256)} %copy-done.31) | copy-start | bytes 3076
  781.5 12.8 %copy-start.35 = (f32[256]{0:T(256)S(1)}, f32[256]{0:T(256)}, u32[]{:S(2)}) copy-start(f32[256]{0:T(256)} %copy-done.34) | copy-start | bytes 3076
  781.5 12.8 %copy-start.36 = (f32[256]{0:T(256)S(1)}, f32[256]{0:T(256)}, u32[]{:S(2)}) copy-start(f32[256]{0:T(256)} %broadcast_multiply_fusion) | copy-start | bytes 3076
  781.5 12.8 %copy-start.37 = (f32[256]{0:T(256)S(1)}, f32[256]{0:T(256)}, u32[]{:S(2)}) copy-start(f32[256]{0:T(256)} %broadcast_multiply_fusion.1) | copy-start | bytes 3076
  782.5 14.3 %copy-start.24 = (f32[6,1024]{1,0:T(8,128)}, f32[6,1024]{1,0:T(8,128)S(1)}, u32[]{:S(2)}) copy-start(f32[6,1024]{1,0:T(8,128)S(1)} %get-tuple-element.260) | copy-start | bytes 73732
  782.5 14.3 %copy-start.25 = (f32[6,1024]{1,0:T(8,128)}, f32[6,1024]{1,0:T(8,128)S(1)}, u32[]{:S(2)}) copy-start(f32[6,1024]{1,0:T(8,128)S(1)} %get-tuple-element.261) | copy-start | bytes 73732
  (14 other events, 32.6 us)
Sparse Core Ops, SparseCore 0:
  10.6 51.4 all-gather.8
  64.3 20.3 all-gather.6
  117.7 44.5 reduce-scatter.8
  164.9 49.1 all-gather.10
  215.4 21.0 all-gather.14
  239.1 49.0 all-gather.12
  302.7 43.1 reduce-scatter.12
  348.4 31.1 reduce-scatter.10
  383.6 22.5 all-gather.16
  409.6 68.4 reduce-scatter.20
  481.6 67.4 reduce-scatter.22
  552.9 61.7 reduce-scatter.18
  618.1 65.3 reduce-scatter.16
  685.8 29.9 reduce-scatter.14
